TPU v7x, 32 devices: a whole 2x2x4 slice. The times are simulated.
32 devices in a mesh: ctx: 8 (over z, x), chan: 2 (over core), dp: 2 (over y).
Axes of the slice: x: 2, y: 2, z: 4, core: 2. Of those that a mesh axis runs over, the one named last changes fastest.
Arguments:
- q_stream: bfloat16 [2, 2048, 4096], P('dp', 'ctx', 'chan'), may hold values from -6 to 6
- k_stream: bfloat16 [2, 2048, 4096], P('dp', 'ctx', 'chan'), may hold values from -6 to 6
- v_stream: bfloat16 [2, 2048, 4096], P('dp', 'ctx', 'chan'), may hold values from -6 to 6
- out_grad: bfloat16 [2, 2048, 4096], P('dp', 'ctx', 'chan'), may hold values from -6 to 6
- norm_gain: float32 [4096], P('chan'), may hold values from 0.1 to 1.9
- residue: float32 [4096, 16], P('chan'), may hold values from -6 to 6
- rate: float32 [4096, 16], P('chan'), may hold values from -1.5 to 6
Outputs:
- y_out: bfloat16 [2, 2048, 4096], P('dp', 'ctx', 'chan')
- grad_q: bfloat16 [2, 2048, 4096], P('dp', 'ctx', 'chan')
- grad_k: bfloat16 [2, 2048, 4096], P('dp', 'ctx', 'chan')
- grad_v: bfloat16 [2, 2048, 4096], P('dp', 'ctx', 'chan')
- grad_residue: float32 [4096, 16], P('chan')
- grad_rate: float32 [4096, 16], P('chan')
- grad_gain: float32 [4096], P('chan')
All inputs are finite; a program needn't handle non-finite values.
Results may differ from a plain program's by a relative error of at most 0.0051.
Values may be sent and summed in bfloat16 or wider, within the bound.
No kernel may reach another device: no remote copies, remote signals or barrier semaphores. Data moves between devices by JAX's collectives and lax.ppermute only.
A program may use at most 128 MiB of HBM per device.

v0:
```python
import math
import jax
import jax.numpy as jnp
from jax import lax
from jax.sharding import PartitionSpec as P

D = 4096
highest = lax.Precision.HIGHEST
epsilon = 1e-06


def modal(decays, angles, parity, seq_len, with_slope):
    shrink = jnp.exp(-decays)[None, :]
    gap_one = (-jnp.expm1(-decays))[None, :]
    tail_val = jnp.exp(-decays * seq_len)[None, :]
    gap_all = (-jnp.expm1(-decays * seq_len))[None, :]
    odd_rows = (parity > 0)[:, None]
    numer = jnp.where(odd_rows, 1.0 + tail_val, gap_all)
    half_sin = jnp.sin(angles * 0.5)[:, None]
    full_sin = jnp.sin(angles)[:, None]
    den_real = gap_one + 2.0 * shrink * half_sin * half_sin
    den_imag = shrink * full_sin
    magnitude = den_real * den_real + den_imag * den_imag
    value_real = numer * den_real / magnitude
    value_imag = -numer * den_imag / magnitude
    if not with_slope:
        return (value_real, value_imag)
    power = jnp.where(odd_rows, -tail_val, tail_val)
    z_real = shrink * jnp.cos(angles)[:, None]
    z_imag = -shrink * full_sin
    top_real = seq_len * power * den_real - numer * z_real
    top_imag = seq_len * power * den_imag - numer * z_imag
    square_real = den_real * den_real - den_imag * den_imag
    square_imag = 2.0 * den_real * den_imag
    quartic = magnitude * magnitude
    slope_real = (top_real * square_real + top_imag * square_imag) / quartic
    slope_imag = (top_imag * square_real - top_real * square_imag) / quartic
    return (value_real, value_imag, slope_real, slope_imag)


def gating(conv, q_part, grad_part, norm_gain):
    q_float = q_part.astype(jnp.float32)
    grad_float = grad_part.astype(jnp.float32)
    mixed = q_float * conv
    scaled = norm_gain * grad_float
    squares, inner_sum = lax.psum(
        (jnp.sum(mixed * mixed, axis=-1), jnp.sum(scaled * mixed, axis=-1)), "chan"
    )
    inv_rms = lax.rsqrt(squares / D + epsilon)[..., None]
    inner_sum = inner_sum[..., None]
    y_part = (norm_gain * mixed * inv_rms).astype(jnp.bfloat16)
    mixed_grad = inv_rms * scaled - mixed * (inv_rms * inv_rms * inv_rms * inner_sum / D)
    grad_q = (mixed_grad * conv).astype(jnp.bfloat16)
    gate_grad = mixed_grad * q_float
    gain_part = jnp.sum((grad_float * mixed * inv_rms).reshape(-1, conv.shape[-1]), axis=0)
    return (y_part, grad_q, gate_grad, gain_part)


def transform_plan(q_stream, k_stream, v_stream, out_grad, norm_gain, residue, rate):
    ctx_count = lax.axis_size("ctx")
    ctx_rank = lax.axis_index("ctx")
    batch_rows, length, channels = q_stream.shape
    slice_len = length // ctx_count
    seq_len = length * ctx_count
    period = 2 * seq_len
    is_first = ctx_rank == 0
    slots = jnp.arange(ctx_count, dtype=jnp.int32)
    slot_angle = (slots[:, None] * slots[None, :] % (2 * ctx_count)).astype(jnp.float32) * (
        math.pi / ctx_count
    )
    signs = (1 - 2 * (slots % 2)).astype(jnp.float32)
    lead_row = slots[:, None] == 0
    lead_col = slots[None, :] == 0
    forward_real = jnp.where(lead_row, 1.0, jnp.cos(slot_angle))
    forward_imag = jnp.where(lead_row, signs[None, :], -jnp.sin(slot_angle))
    inverse_real = jnp.where(lead_col, 1.0, 2.0 * jnp.cos(slot_angle)) / period
    inverse_imag = jnp.where(lead_col, signs[:, None], -2.0 * jnp.sin(slot_angle)) / period
    columns = jnp.arange(length, dtype=jnp.int32)
    freq_a = jnp.where(is_first, 0, ctx_rank) + 2 * ctx_count * columns
    freq_b = jnp.where(is_first, ctx_count, ctx_rank) + 2 * ctx_count * columns

    def twiddle(freq):
        phase = (freq[:, None] * columns[None, :] % period).astype(jnp.float32) * (
            2.0 * math.pi / period
        )
        return (jnp.cos(phase), jnp.sin(phase))

    cosine_a, sine_a = twiddle(freq_a)
    cosine_b, sine_b = twiddle(freq_b)
    angles_a = freq_a.astype(jnp.float32) * (2.0 * math.pi / period)
    angles_b = freq_b.astype(jnp.float32) * (2.0 * math.pi / period)
    parity_a = freq_a % 2
    parity_b = freq_b % 2

    def spectrum(slices):
        slot_real = jnp.einsum("kb,xbjc->xkjc", forward_real, slices, precision=highest)
        slot_imag = jnp.einsum("kb,xbjc->xkjc", forward_imag, slices, precision=highest)
        rows_real, rows_imag = (
            lax.all_to_all(slot_real, "ctx", split_axis=1, concat_axis=1, tiled=True),
            lax.all_to_all(slot_imag, "ctx", split_axis=1, concat_axis=1, tiled=True),
        )
        rows_real = rows_real.reshape(batch_rows, length, channels)
        rows_imag = rows_imag.reshape(batch_rows, length, channels)
        a_real = jnp.einsum("kj,xjc->xkc", cosine_a, rows_real, precision=highest)
        a_imag = -jnp.einsum("kj,xjc->xkc", sine_a, rows_real, precision=highest)
        b_real = jnp.einsum("kj,xjc->xkc", cosine_b, rows_imag, precision=highest)
        b_imag = -jnp.einsum("kj,xjc->xkc", sine_b, rows_imag, precision=highest)
        return (a_real, a_imag, b_real, b_imag)

    def positions(spec):
        g_ar, g_ai, g_br, g_bi = spec
        u_first = g_ar - g_bi
        u_second = g_ai + g_br
        x_first = jnp.where(is_first, g_ar, u_first)
        x_second = jnp.where(is_first, g_ai, u_second)
        y_first = jnp.where(is_first, g_br, u_second)
        y_second = jnp.where(is_first, -g_bi, u_first)
        out_real = jnp.einsum("kj,xkc->xjc", cosine_a, x_first, precision=highest) - jnp.einsum(
            "kj,xkc->xjc", sine_a, x_second, precision=highest
        )
        out_imag = jnp.einsum("kj,xkc->xjc", cosine_b, y_first, precision=highest) + jnp.einsum(
            "kj,xkc->xjc", sine_b, y_second, precision=highest
        )
        out_real = out_real.reshape(batch_rows, ctx_count, slice_len, channels)
        out_imag = out_imag.reshape(batch_rows, ctx_count, slice_len, channels)
        recv_real, recv_imag = (
            lax.all_to_all(out_real, "ctx", split_axis=1, concat_axis=1, tiled=True),
            lax.all_to_all(out_imag, "ctx", split_axis=1, concat_axis=1, tiled=True),
        )
        return jnp.einsum("bk,xkjc->xbjc", inverse_real, recv_real, precision=highest) + jnp.einsum(
            "bk,xkjc->xbjc", inverse_imag, recv_imag, precision=highest
        )

    def multiply(spec, kernel_rows, flip):
        s_ar, s_ai, s_br, s_bi = spec
        h_ar, h_ai, h_br, h_bi = kernel_rows
        if flip:
            h_ai = -h_ai
            h_bi = -h_bi
        return (
            s_ar * h_ar - s_ai * h_ai,
            s_ai * h_ar + s_ar * h_ai,
            s_br * h_br - s_bi * h_bi,
            s_bi * h_br + s_br * h_bi,
        )

    decays = jnp.exp(rate) / seq_len
    flat_decays = decays.reshape(-1)
    mode_count = residue.shape[1]
    block = math.gcd(length, 64)
    block_count = length // block
    block_ids = jnp.arange(block_count, dtype=jnp.int32)

    def kernel_block(carry, block_index):
        row_start = block_index * block
        pieces_now = []
        for angles, parity in ((angles_a, parity_a), (angles_b, parity_b)):
            angle_rows = lax.dynamic_slice_in_dim(angles, row_start, block)
            parity_rows = lax.dynamic_slice_in_dim(parity, row_start, block)
            f_real, f_imag = modal(flat_decays, angle_rows, parity_rows, seq_len, False)
            pieces_now.append(
                jnp.sum(f_real.reshape(block, channels, mode_count) * residue, axis=-1)
            )
            pieces_now.append(
                jnp.sum(f_imag.reshape(block, channels, mode_count) * residue, axis=-1)
            )
        return (carry, tuple(pieces_now))

    _, kernel_pieces = lax.scan(kernel_block, 0.0, block_ids)
    kernel_rows = tuple((piece.reshape(length, channels) for piece in kernel_pieces))
    value_blocks = (k_stream.astype(jnp.float32) * v_stream.astype(jnp.float32)).astype(
        jnp.bfloat16
    )
    value_sl = lax.all_to_all(
        value_blocks.reshape(batch_rows, ctx_count, slice_len, channels),
        "ctx",
        split_axis=1,
        concat_axis=1,
        tiled=True,
    ).astype(jnp.float32)
    value_spec = spectrum(value_sl)
    conv_sl = positions(multiply(value_spec, kernel_rows, False))
    conv_blk = lax.all_to_all(conv_sl, "ctx", split_axis=1, concat_axis=1, tiled=True).reshape(
        batch_rows, length, channels
    )
    y_out, grad_q, gate_blk, gain_part = gating(conv_blk, q_stream, out_grad, norm_gain)
    gate_sl = lax.all_to_all(
        gate_blk.reshape(batch_rows, ctx_count, slice_len, channels),
        "ctx",
        split_axis=1,
        concat_axis=1,
        tiled=True,
    )
    gate_spec = spectrum(gate_sl)
    grad_sl = positions(multiply(gate_spec, kernel_rows, True))
    value_grad = lax.all_to_all(grad_sl, "ctx", split_axis=1, concat_axis=1, tiled=True).reshape(
        batch_rows, length, channels
    )
    grad_k = (value_grad * v_stream.astype(jnp.float32)).astype(jnp.bfloat16)
    grad_v = (value_grad * k_stream.astype(jnp.float32)).astype(jnp.bfloat16)

    def true_rows(spec):
        s_ar, s_ai, s_br, s_bi = spec
        return (
            jnp.where(is_first, s_ar, s_ar - s_bi),
            jnp.where(is_first, s_ai, s_ai + s_br),
            s_br,
            s_bi,
        )

    z_ar, z_ai, z_br, z_bi = true_rows(value_spec)
    g_ar, g_ai, g_br, g_bi = true_rows(gate_spec)
    cross_ar = jnp.sum(g_ar * z_ar + g_ai * z_ai, axis=0)
    cross_ai = jnp.sum(g_ai * z_ar - g_ar * z_ai, axis=0)
    cross_br = jnp.sum(g_br * z_br + g_bi * z_bi, axis=0)
    cross_bi = jnp.sum(g_bi * z_br - g_br * z_bi, axis=0)
    weight_a = jnp.where(is_first, 1.0, 2.0) / period
    weight_b = jnp.where(is_first, 1.0, 0.0) / period

    def grad_block(totals, block_index):
        row_start = block_index * block
        sums_now = []
        for angles, parity, cross_real, cross_imag in (
            (angles_a, parity_a, cross_ar, cross_ai),
            (angles_b, parity_b, cross_br, cross_bi),
        ):
            angle_rows = lax.dynamic_slice_in_dim(angles, row_start, block)
            parity_rows = lax.dynamic_slice_in_dim(parity, row_start, block)
            real_rows = lax.dynamic_slice_in_dim(cross_real, row_start, block)[:, :, None]
            imag_rows = lax.dynamic_slice_in_dim(cross_imag, row_start, block)[:, :, None]
            f_real, f_imag, d_real, d_imag = modal(
                flat_decays, angle_rows, parity_rows, seq_len, True
            )
            shape_three = (block, channels, mode_count)
            sums_now.append(
                jnp.sum(
                    real_rows * f_real.reshape(shape_three)
                    + imag_rows * f_imag.reshape(shape_three),
                    axis=0,
                )
            )
            sums_now.append(
                jnp.sum(
                    real_rows * d_real.reshape(shape_three)
                    + imag_rows * d_imag.reshape(shape_three),
                    axis=0,
                )
            )
        return (tuple((total + part for total, part in zip(totals, sums_now))), None)

    zero_modes = jnp.zeros((channels, mode_count), jnp.float32)
    (res_a, slope_a, res_b, slope_b), _ = lax.scan(
        grad_block, (zero_modes, zero_modes, zero_modes, zero_modes), block_ids
    )
    res_part = weight_a * res_a + weight_b * res_b
    rate_part = decays * residue * (weight_a * slope_a + weight_b * slope_b)
    return (y_out, grad_q, grad_k, grad_v, res_part, rate_part, gain_part)


def shards(q_stream, k_stream, v_stream, out_grad, norm_gain, residue, rate):
    results = transform_plan(q_stream, k_stream, v_stream, out_grad, norm_gain, residue, rate)
    y_out, grad_q, grad_k, grad_v, res_part, rate_part, gain_part = results
    grad_residue, grad_rate, grad_gain = lax.psum((res_part, rate_part, gain_part), ("ctx", "dp"))
    return (y_out, grad_q, grad_k, grad_v, grad_residue, grad_rate, grad_gain)


def solution(mesh):
    in_specs = (
        P("dp", "ctx", "chan"),
        P("dp", "ctx", "chan"),
        P("dp", "ctx", "chan"),
        P("dp", "ctx", "chan"),
        P("chan"),
        P("chan", None),
        P("chan", None),
    )
    out_specs = (
        P("dp", "ctx", "chan"),
        P("dp", "ctx", "chan"),
        P("dp", "ctx", "chan"),
        P("dp", "ctx", "chan"),
        P("chan", None),
        P("chan", None),
        P("chan"),
    )
    return jax.shard_map(shards, mesh=mesh, in_specs=in_specs, out_specs=out_specs, check_vma=False)
```

profile of v0, /device:TPU:0, one launch (start us, length us, event | category | flops | bytes accessed | tf_op | source)
XLA Modules:
  0.0 1118.8 jit_solution(14108941958894904162)
XLA Ops:
  10.1 7.3 all-to-all-start
  18.8 24.3 %all-to-all-done = bf16[1,8,32,2048]{3,2,0,1:T(8,128)(2,1)S(1)} async-done(((bf16[1,8,32,2048]{3,2,0,1:T(8,128)(2,1)}), bf16[1,8,32,2048]{3,2,0,1:T(8,128)(2,1)S(1)}, u32[]{:S(2)}, u32[]{:S(2)}) %all-to-all-start) | async-done | bytes 1048608 | tf_op jit(solution)/shard_map/all_to_all | solution.py:174
  57.4 41.7 %all-to-all-done.2 = f32[1,8,32,2048]{3,2,0,1:T(8,128)S(1)} async-done(((f32[1,8,32,2048]{3,2,0,1:T(8,128)}), f32[1,8,32,2048]{3,2,0,1:T(8,128)S(1)}, u32[]{:S(2)}, u32[]{:S(2)}) %all-to-all-start.2) | async-done | bytes 2097184 | tf_op jit(solution)/shard_map/all_to_all | solution.py:100
  99.1 4.6 all-to-all-start.1
  103.7 114.4 %while.39 = (s32[]{:T(128)}, f32[4,64,2048]{2,1,0:T(8,128)}, f32[4,64,2048]{2,1,0:T(8,128)}, f32[4,64,2048]{2,1,0:T(8,128)}, f32[4,64,2048]{2,1,0:T(8,128)}, /*i...) while((s32[]{:T(128)}, f32[4,64,2048]{2,1,0:T(8,128)}, ...), condition=%wide.region_5.6_spmd, body=%wide.region_0.5_spmd.sunk | while | flops 70910216 | bytes 10621447 | solution.py:169
  115.0 15.1 %fusion.311 = (f32[64,2048]{1,0:T(8,128)S(1)}, f32[64,2048]{1,0:T(8,128)S(1)}, f32[64,2048]{1,0:T(8,128)S(1)}, f32[64,2048]{1,0:T(8,128)S(1)}) fusion(f32[64]{0:T(128)S(1)} %get-tuple-element.922, f32[64]{0:T(128)S(1)} %get-tuple-element.923, f32[2048,16]{0,1:T(8,128)S(1)} %get-tuple-element.1021, f32[2048,16]{0,1:T(8,128)S(1)} %copy.198, ...), kind=kLoop, calls=%fused_computation.19.clone.1 | loop fusion | flops 70778880 | bytes 2884736 | tf_op jit(solution)/shard_map/while/body/eval_jaxpr/reduce_sum | solution.py:165
  143.7 15.1 %fusion.311 = (f32[64,2048]{1,0:T(8,128)S(1)}, f32[64,2048]{1,0:T(8,128)S(1)}, f32[64,2048]{1,0:T(8,128)S(1)}, f32[64,2048]{1,0:T(8,128)S(1)}) fusion(f32[64]{0:T(128)S(1)} %get-tuple-element.922, f32[64]{0:T(128)S(1)} %get-tuple-element.923, f32[2048,16]{0,1:T(8,128)S(1)} %get-tuple-element.1021, f32[2048,16]{0,1:T(8,128)S(1)} %copy.198, ...), kind=kLoop, calls=%fused_computation.19.clone.1 | loop fusion | flops 70778880 | bytes 2884736 | tf_op jit(solution)/shard_map/while/body/eval_jaxpr/reduce_sum | solution.py:165
  172.2 15.1 %fusion.311 = (f32[64,2048]{1,0:T(8,128)S(1)}, f32[64,2048]{1,0:T(8,128)S(1)}, f32[64,2048]{1,0:T(8,128)S(1)}, f32[64,2048]{1,0:T(8,128)S(1)}) fusion(f32[64]{0:T(128)S(1)} %get-tuple-element.922, f32[64]{0:T(128)S(1)} %get-tuple-element.923, f32[2048,16]{0,1:T(8,128)S(1)} %get-tuple-element.1021, f32[2048,16]{0,1:T(8,128)S(1)} %copy.198, ...), kind=kLoop, calls=%fused_computation.19.clone.1 | loop fusion | flops 70778880 | bytes 2884736 | tf_op jit(solution)/shard_map/while/body/eval_jaxpr/reduce_sum | solution.py:165
  200.8 15.1 %fusion.311 = (f32[64,2048]{1,0:T(8,128)S(1)}, f32[64,2048]{1,0:T(8,128)S(1)}, f32[64,2048]{1,0:T(8,128)S(1)}, f32[64,2048]{1,0:T(8,128)S(1)}) fusion(f32[64]{0:T(128)S(1)} %get-tuple-element.922, f32[64]{0:T(128)S(1)} %get-tuple-element.923, f32[2048,16]{0,1:T(8,128)S(1)} %get-tuple-element.1021, f32[2048,16]{0,1:T(8,128)S(1)} %copy.198, ...), kind=kLoop, calls=%fused_computation.19.clone.1 | loop fusion | flops 70778880 | bytes 2884736 | tf_op jit(solution)/shard_map/while/body/eval_jaxpr/reduce_sum | solution.py:165
  229.2 5.9 convolution_bitcast_fusion.7
  235.2 6.7 fusion.38
  241.9 8.5 multiply_subtract_fusion.2
  250.4 9.0 multiply_add_fusion.6
  262.7 4.8 convolution_subtract_fusion.1
  267.5 6.1 all-to-all-start.3
  273.6 4.9 fusion.51
  278.6 4.7 convolution_add_fusion.3
  283.2 37.7 %all-to-all-done.3 = f32[1,8,32,2048]{3,2,0,1:T(8,128)} async-done(((f32[1,8,32,2048]{3,2,0,1:T(8,128)}), f32[1,8,32,2048]{3,2,0,1:T(8,128)}, u32[]{:S(2)}, u32[]{:S(2)}) %all-to-all-start.3) | async-done | bytes 2097184 | tf_op jit(solution)/shard_map/all_to_all | solution.py:127
  325.0 6.2 fusion.68
  331.2 42.2 %all-to-all-done.4 = f32[1,8,32,2048]{3,2,0,1:T(8,128)S(1)} async-done(((f32[1,8,32,2048]{3,2,0,1:T(8,128)}), f32[1,8,32,2048]{3,2,0,1:T(8,128)S(1)}, u32[]{:S(2)}, u32[]{:S(2)}) %all-to-all-start.4) | async-done | bytes 2097184 | tf_op jit(solution)/shard_map/all_to_all | solution.py:128
  373.3 4.9 fusion.37
  379.5 51.9 %all_to_all.60 = f32[1,8,32,2048]{3,2,0,1:T(8,128)S(1)} all-to-all(f32[1,8,32,2048]{3,2,0,1:T(8,128)S(1)} %copy.131), channel_id=1, replica_groups=mesh['ctx'=8,'chan'=2,'dp'=2] {'ctx'}, dimensions={1} | all-to-all | bytes 4194304 | tf_op jit(solution)/shard_map/all_to_all | solution.py:183
  442.2 52.1 %all_to_all.61 = f32[1,8,32,2048]{3,2,0,1:T(8,128)S(1)} all-to-all(f32[1,8,32,2048]{3,2,0,1:T(8,128)S(1)} %bitcast.214), channel_id=1, replica_groups=mesh['ctx'=8,'chan'=2,'dp'=2] {'ctx'}, dimensions={1} | all-to-all | bytes 4194304 | tf_op jit(solution)/shard_map/all_to_all | solution.py:187
  510.3 41.6 %all-to-all-done.8 = f32[1,8,32,2048]{3,2,0,1:T(8,128)} async-done(((f32[1,8,32,2048]{3,2,0,1:T(8,128)}), f32[1,8,32,2048]{3,2,0,1:T(8,128)}, u32[]{:S(2)}, u32[]{:S(2)}) %all-to-all-start.8) | async-done | bytes 2097184 | tf_op jit(solution)/shard_map/all_to_all | solution.py:100
  555.7 7.2 convolution_bitcast_fusion
  562.9 7.3 convolution_bitcast_fusion.1
  570.2 33.8 %all-to-all-done.7 = f32[1,8,32,2048]{3,2,0,1:T(8,128)S(1)} async-done(((f32[1,8,32,2048]{3,2,0,1:T(8,128)}), f32[1,8,32,2048]{3,2,0,1:T(8,128)S(1)}, u32[]{:S(2)}, u32[]{:S(2)}) %all-to-all-start.7) | async-done | bytes 2097184 | tf_op jit(solution)/shard_map/all_to_all | solution.py:99
  603.9 5.9 convolution_bitcast_fusion.3
  609.8 18.4 %subtract_bitcast_fusion.1 = (f32[256,2048]{0,1:T(8,128)}, f32[256,2048]{0,1:T(8,128)}, f32[256,2048]{0,1:T(8,128)}, f32[256,2048]{0,1:T(8,128)}, f32[1,256,2048...) fusion(f32[1,256,2048]{1,2,0:T(8,128)} %copy-done.9, ...), kind=kOutput, calls=%fused_computation.170 | convolution fusion | flops 1630928896 | bytes 41944064 | tf_op jit(solution)/shard_map/kj,xjc->xkc/dot_general | solution.py:104
  631.5 4.6 convolution_subtract_fusion
  636.0 4.5 all-to-all-start.9
  640.6 5.6 fusion.56
  646.1 4.7 convolution_add_fusion.1
  650.8 37.5 %all-to-all-done.9 = f32[1,8,32,2048]{3,2,0,1:T(8,128)} async-done(((f32[1,8,32,2048]{3,2,0,1:T(8,128)}), f32[1,8,32,2048]{3,2,0,1:T(8,128)}, u32[]{:S(2)}, u32[]{:S(2)}) %all-to-all-start.9) | async-done | bytes 2097184 | tf_op jit(solution)/shard_map/all_to_all | solution.py:127
  692.8 69.5 %psum.39 = f32[2048]{0:T(1024)} all-reduce(f32[2048]{0:T(1024)S(1)} %get-tuple-element.596), channel_id=1, replica_groups=mesh['ctx'=8,'chan'=2,'dp'=2] {'ctx','dp'}, use_global_device_ids=true, to_apply=%region_19.20 | all-reduce | flops 2048 | bytes 16384 | tf_op jit(solution)/shard_map/psum | solution.py:263
  772.1 6.2 fusion.60
  778.3 5.5 fusion.36
  786.3 7.2 all-to-all-start.11
  794.2 203.1 %while.40 = (s32[]{:T(128)}, f32[2048,16]{0,1:T(8,128)}, f32[2048,16]{0,1:T(8,128)}, f32[2048,16]{0,1:T(8,128)}, f32[2048,16]{0,1:T(8,128)}, /*index=5*/s32[4]{0...) while((s32[]{:T(128)}, f32[2048,16]{0,1:T(8,128)}, ...), condition=%wide.region_15.16_spmd.clone, body=%wide.region_10.15_spmd.clone.sunk | while | flops 180650240 | bytes 40907724 | solution.py:252
  812.7 13.5 %add_reduce_fusion.8 = (f32[2048,16]{0,1:T(8,128)S(1)}, f32[2048,16]{0,1:T(8,128)S(1)}) fusion(f32[64]{0:T(128)S(1)} %get-tuple-element.965, f32[64,2048]{1,0:T(8,128)S(1)} %copy-done, f32[64]{0:T(128)S(1)} %get-tuple-element.966, f32[64]{0:T(128)S(1)} %get-tuple-element.967, f32[64,2048]{1,0:T(8,128)S(1)} %copy-done.1, f32[2048,16]{0,1:T(8,128)S(1)} %copy.203, ...), kind=kLoop, calls=%fused_computation.71.clone.1 | loop fusion | flops 90112000 | bytes 2360128 | tf_op jit(solution)/shard_map/while/body/eval_jaxpr/reduce_sum | solution.py:243
  830.1 12.9 %add_reduce_fusion.7 = (f32[2048,16]{0,1:T(8,128)S(1)}, f32[2048,16]{0,1:T(8,128)S(1)}) fusion(f32[2048,16]{0,1:T(8,128)S(1)} %copy.203, f32[64]{0:T(128)S(1)} %get-tuple-element.954, f32[2048,16]{0,1:T(8,128)S(1)} %copy.204, f32[2048,16]{0,1:T(8,128)S(1)} %copy.205, f32[64,2048]{1,0:T(8,128)S(1)} %constant_dynamic-slice_fusion.8, ...), kind=kLoop, calls=%fused_computation.75.clone.1 | loop fusion | flops 90112000 | bytes 2360128 | tf_op jit(solution)/shard_map/while/body/eval_jaxpr/reduce_sum | solution.py:243
  862.8 13.5 %add_reduce_fusion.8 = (f32[2048,16]{0,1:T(8,128)S(1)}, f32[2048,16]{0,1:T(8,128)S(1)}) fusion(f32[64]{0:T(128)S(1)} %get-tuple-element.965, f32[64,2048]{1,0:T(8,128)S(1)} %copy-done, f32[64]{0:T(128)S(1)} %get-tuple-element.966, f32[64]{0:T(128)S(1)} %get-tuple-element.967, f32[64,2048]{1,0:T(8,128)S(1)} %copy-done.1, f32[2048,16]{0,1:T(8,128)S(1)} %copy.203, ...), kind=kLoop, calls=%fused_computation.71.clone.1 | loop fusion | flops 90112000 | bytes 2360128 | tf_op jit(solution)/shard_map/while/body/eval_jaxpr/reduce_sum | solution.py:243
  881.1 12.9 %add_reduce_fusion.7 = (f32[2048,16]{0,1:T(8,128)S(1)}, f32[2048,16]{0,1:T(8,128)S(1)}) fusion(f32[2048,16]{0,1:T(8,128)S(1)} %copy.203, f32[64]{0:T(128)S(1)} %get-tuple-element.954, f32[2048,16]{0,1:T(8,128)S(1)} %copy.204, f32[2048,16]{0,1:T(8,128)S(1)} %copy.205, f32[64,2048]{1,0:T(8,128)S(1)} %constant_dynamic-slice_fusion.8, ...), kind=kLoop, calls=%fused_computation.75.clone.1 | loop fusion | flops 90112000 | bytes 2360128 | tf_op jit(solution)/shard_map/while/body/eval_jaxpr/reduce_sum | solution.py:243
  913.7 13.5 %add_reduce_fusion.8 = (f32[2048,16]{0,1:T(8,128)S(1)}, f32[2048,16]{0,1:T(8,128)S(1)}) fusion(f32[64]{0:T(128)S(1)} %get-tuple-element.965, f32[64,2048]{1,0:T(8,128)S(1)} %copy-done, f32[64]{0:T(128)S(1)} %get-tuple-element.966, f32[64]{0:T(128)S(1)} %get-tuple-element.967, f32[64,2048]{1,0:T(8,128)S(1)} %copy-done.1, f32[2048,16]{0,1:T(8,128)S(1)} %copy.203, ...), kind=kLoop, calls=%fused_computation.71.clone.1 | loop fusion | flops 90112000 | bytes 2360128 | tf_op jit(solution)/shard_map/while/body/eval_jaxpr/reduce_sum | solution.py:243
  932.0 12.9 %add_reduce_fusion.7 = (f32[2048,16]{0,1:T(8,128)S(1)}, f32[2048,16]{0,1:T(8,128)S(1)}) fusion(f32[2048,16]{0,1:T(8,128)S(1)} %copy.203, f32[64]{0:T(128)S(1)} %get-tuple-element.954, f32[2048,16]{0,1:T(8,128)S(1)} %copy.204, f32[2048,16]{0,1:T(8,128)S(1)} %copy.205, f32[64,2048]{1,0:T(8,128)S(1)} %constant_dynamic-slice_fusion.8, ...), kind=kLoop, calls=%fused_computation.75.clone.1 | loop fusion | flops 90112000 | bytes 2360128 | tf_op jit(solution)/shard_map/while/body/eval_jaxpr/reduce_sum | solution.py:243
  964.6 13.5 %add_reduce_fusion.8 = (f32[2048,16]{0,1:T(8,128)S(1)}, f32[2048,16]{0,1:T(8,128)S(1)}) fusion(f32[64]{0:T(128)S(1)} %get-tuple-element.965, f32[64,2048]{1,0:T(8,128)S(1)} %copy-done, f32[64]{0:T(128)S(1)} %get-tuple-element.966, f32[64]{0:T(128)S(1)} %get-tuple-element.967, f32[64,2048]{1,0:T(8,128)S(1)} %copy-done.1, f32[2048,16]{0,1:T(8,128)S(1)} %copy.203, ...), kind=kLoop, calls=%fused_computation.71.clone.1 | loop fusion | flops 90112000 | bytes 2360128 | tf_op jit(solution)/shard_map/while/body/eval_jaxpr/reduce_sum | solution.py:243
  982.9 12.9 %add_reduce_fusion.7 = (f32[2048,16]{0,1:T(8,128)S(1)}, f32[2048,16]{0,1:T(8,128)S(1)}) fusion(f32[2048,16]{0,1:T(8,128)S(1)} %copy.203, f32[64]{0:T(128)S(1)} %get-tuple-element.954, f32[2048,16]{0,1:T(8,128)S(1)} %copy.204, f32[2048,16]{0,1:T(8,128)S(1)} %copy.205, f32[64,2048]{1,0:T(8,128)S(1)} %constant_dynamic-slice_fusion.8, ...), kind=kLoop, calls=%fused_computation.75.clone.1 | loop fusion | flops 90112000 | bytes 2360128 | tf_op jit(solution)/shard_map/while/body/eval_jaxpr/reduce_sum | solution.py:243
  1004.8 103.6 %all-reduce.3.cloned.1.call-done = (f32[2048,16]{0,1:T(8,128)}, f32[2048,16]{0,1:T(8,128)}) async-done(((f32[2048,16]{0,1:T(8,128)}, f32[2048,16]{0,1:T(8,128)}), (f32[2048,16]{0,1:T(8,128)}, f32[2048,16]{0,1:T(8,128)})) %all-reduce.3.cloned.1.call-update) | async-done | bytes 262160 | tf_op jit(solution)/shard_map/psum | solution.py:263
  (439 shorter events, 244.7 us)
Async XLA Ops:
  7.2 10.2 copy-start.36
  10.1 33.0 %all-to-all-start = ((bf16[1,8,32,2048]{3,2,0,1:T(8,128)(2,1)}), bf16[1,8,32,2048]{3,2,0,1:T(8,128)(2,1)S(1)}, u32[]{:S(2)}, u32[]{:S(2)}) async-start(bf16[1,8,32,2048]{3,2,0,1:T(8,128)(2,1)} %bitcast.6), calls=%async_computation | async-start | bytes 2097152 | tf_op jit(solution)/shard_map/all_to_all | solution.py:174
  47.1 52.0 %all-to-all-start.2 = ((f32[1,8,32,2048]{3,2,0,1:T(8,128)}), f32[1,8,32,2048]{3,2,0,1:T(8,128)S(1)}, u32[]{:S(2)}, u32[]{:S(2)}) async-start(f32[1,8,32,2048]{3,2,0,1:T(8,128)} %copy.120), calls=%async_computation.2 | async-start | bytes 4194304 | tf_op jit(solution)/shard_map/all_to_all | solution.py:100
  57.4 46.3 %copy-start.27 = (f32[2048,16]{0,1:T(8,128)S(1)}, f32[2048,16]{0,1:T(8,128)}, u32[]{:S(2)}) copy-start(f32[2048,16]{0,1:T(8,128)} %param.16) | copy-start | bytes 393220
  99.1 136.0 %all-to-all-start.1 = ((f32[1,8,32,2048]{3,2,0,1:T(8,128)}), f32[1,8,32,2048]{3,2,0,1:T(8,128)}, u32[]{:S(2)}, u32[]{:S(2)}) async-start(f32[1,8,32,2048]{3,2,0,1:T(8,128)} %copy.116), calls=%async_computation.1 | async-start | bytes 4194304 | tf_op jit(solution)/shard_map/all_to_all | solution.py:99
  235.1 6.7 copy-start.7
  235.1 6.7 copy-start.10
  235.2 6.7 copy-start.11
  241.9 8.5 copy-start.9
  241.9 8.5 copy-start.12
  241.9 8.5 copy-start.13
  250.4 9.0 copy-start.14
  250.4 12.2 %copy-start.16 = (f32[1,256,2048]{1,2,0:T(8,128)}, f32[1,256,2048]{1,2,0:T(8,128)S(1)}, u32[]{:S(2)}) copy-start(f32[1,256,2048]{1,2,0:T(8,128)S(1)} %get-tuple-element.692) | copy-start | bytes 6291460
  267.5 6.1 copy-start.17
  267.5 53.4 %all-to-all-start.3 = ((f32[1,8,32,2048]{3,2,0,1:T(8,128)}), f32[1,8,32,2048]{3,2,0,1:T(8,128)}, u32[]{:S(2)}, u32[]{:S(2)}) async-start(f32[1,8,32,2048]{3,2,0,1:T(8,128)} %bitcast.213), calls=%async_computation.3 | async-start | bytes 4194304 | tf_op jit(solution)/shard_map/all_to_all | solution.py:127
  320.9 52.4 %all-to-all-start.4 = ((f32[1,8,32,2048]{3,2,0,1:T(8,128)}), f32[1,8,32,2048]{3,2,0,1:T(8,128)S(1)}, u32[]{:S(2)}, u32[]{:S(2)}) async-start(f32[1,8,32,2048]{3,2,0,1:T(8,128)} %bitcast.44), calls=%async_computation.4 | async-start | bytes 4194304 | tf_op jit(solution)/shard_map/all_to_all | solution.py:128
  379.4 52.0 %copy-start.25 = (bf16[1,256,2048]{2,1,0:T(8,128)(2,1)S(1)}, bf16[1,256,2048]{2,1,0:T(8,128)(2,1)}, u32[]{:S(2)}) copy-start(bf16[1,256,2048]{2,1,0:T(8,128)(2,1)} %param.11) | copy-start | bytes 3145732
  500.1 51.8 %all-to-all-start.8 = ((f32[1,8,32,2048]{3,2,0,1:T(8,128)}), f32[1,8,32,2048]{3,2,0,1:T(8,128)}, u32[]{:S(2)}, u32[]{:S(2)}) async-start(f32[1,8,32,2048]{3,2,0,1:T(8,128)} %copy.137), calls=%async_computation.8 | async-start | bytes 4194304 | tf_op jit(solution)/shard_map/all_to_all | solution.py:100
  551.9 52.0 %all-to-all-start.7 = ((f32[1,8,32,2048]{3,2,0,1:T(8,128)}), f32[1,8,32,2048]{3,2,0,1:T(8,128)S(1)}, u32[]{:S(2)}, u32[]{:S(2)}) async-start(f32[1,8,32,2048]{3,2,0,1:T(8,128)} %copy.134), calls=%async_computation.7 | async-start | bytes 4194304 | tf_op jit(solution)/shard_map/all_to_all | solution.py:99
  628.2 7.8 copy-start.4
  628.2 7.8 copy-start.5
  636.0 52.3 %all-to-all-start.9 = ((f32[1,8,32,2048]{3,2,0,1:T(8,128)}), f32[1,8,32,2048]{3,2,0,1:T(8,128)}, u32[]{:S(2)}, u32[]{:S(2)}) async-start(f32[1,8,32,2048]{3,2,0,1:T(8,128)} %bitcast.212), calls=%async_computation.9 | async-start | bytes 4194304 | tf_op jit(solution)/shard_map/all_to_all | solution.py:127
  688.4 89.9 %all-to-all-start.10 = ((f32[1,8,32,2048]{3,2,0,1:T(8,128)}), f32[1,8,32,2048]{3,2,0,1:T(8,128)}, u32[]{:S(2)}, u32[]{:S(2)}) async-start(f32[1,8,32,2048]{3,2,0,1:T(8,128)} %bitcast.211), calls=%async_computation.10 | async-start | bytes 4194304 | tf_op jit(solution)/shard_map/all_to_all | solution.py:128
  786.3 214.4 %all-to-all-start.11 = ((f32[1,8,32,2048]{3,2,0,1:T(8,128)}), f32[1,8,32,2048]{3,2,0,1:T(8,128)}, u32[]{:S(2)}, u32[]{:S(2)}) async-start(f32[1,8,32,2048]{3,2,0,1:T(8,128)} %copy.148), calls=%async_computation.11 | async-start | bytes 4194304 | tf_op jit(solution)/shard_map/all_to_all | solution.py:196
  793.5 314.8 %all-reduce.3.cloned.1.call-start = ((), (), s32[]{:S(2)}) async-start(), calls=%async_computation.12 | async-start | bytes 524288 | tf_op jit(solution)/shard_map/psum | solution.py:263
  794.4 6.0 copy-start.23
  812.1 14.2 %copy-start.33 = (f32[2048,16]{0,1:T(8,128)S(1)}, f32[2048,16]{0,1:T(8,128)}, u32[]{:S(2)}) copy-start(f32[2048,16]{0,1:T(8,128)} %get-tuple-element.1055) | copy-start | bytes 393220 | tf_op jit(solution)/shard_map/while
  812.7 14.3 %copy-start.38 = (f32[256]{0:T(256)S(1)}, f32[256]{0:T(256)}, u32[]{:S(2)}) copy-start(f32[256]{0:T(256)} %get-tuple-element.1086) | copy-start | bytes 3076 | tf_op jit(solution)/shard_map/while
  827.7 15.4 %copy-start.29 = (f32[2048,16]{0,1:T(8,128)S(1)}, f32[2048,16]{0,1:T(8,128)}, u32[]{:S(2)}) copy-start(f32[2048,16]{0,1:T(8,128)} %get-tuple-element.1053) | copy-start | bytes 393220 | tf_op jit(solution)/shard_map/while
  827.7 15.4 %copy-start.31 = (f32[2048,16]{0,1:T(8,128)S(1)}, f32[2048,16]{0,1:T(8,128)}, u32[]{:S(2)}) copy-start(f32[2048,16]{0,1:T(8,128)} %get-tuple-element.1054) | copy-start | bytes 393220 | tf_op jit(solution)/shard_map/while
  828.8 15.7 %copy-start.24 = (f32[256,2048]{1,0:T(8,128)S(1)}, f32[256,2048]{1,0:T(8,128)}, u32[]{:S(2)}) copy-start(f32[256,2048]{1,0:T(8,128)} %copy-done.23) | copy-start | bytes 6291460 | tf_op jit(solution)/shard_map/while
  844.4 6.0 copy-start.23
  862.1 14.2 %copy-start.33 = (f32[2048,16]{0,1:T(8,128)S(1)}, f32[2048,16]{0,1:T(8,128)}, u32[]{:S(2)}) copy-start(f32[2048,16]{0,1:T(8,128)} %get-tuple-element.1055) | copy-start | bytes 393220 | tf_op jit(solution)/shard_map/while
  862.7 15.2 %copy-start.38 = (f32[256]{0:T(256)S(1)}, f32[256]{0:T(256)}, u32[]{:S(2)}) copy-start(f32[256]{0:T(256)} %get-tuple-element.1086) | copy-start | bytes 3076 | tf_op jit(solution)/shard_map/while
  878.6 15.4 %copy-start.29 = (f32[2048,16]{0,1:T(8,128)S(1)}, f32[2048,16]{0,1:T(8,128)}, u32[]{:S(2)}) copy-start(f32[2048,16]{0,1:T(8,128)} %get-tuple-element.1053) | copy-start | bytes 393220 | tf_op jit(solution)/shard_map/while
  878.6 15.4 %copy-start.31 = (f32[2048,16]{0,1:T(8,128)S(1)}, f32[2048,16]{0,1:T(8,128)}, u32[]{:S(2)}) copy-start(f32[2048,16]{0,1:T(8,128)} %get-tuple-element.1054) | copy-start | bytes 393220 | tf_op jit(solution)/shard_map/while
  879.7 15.7 %copy-start.24 = (f32[256,2048]{1,0:T(8,128)S(1)}, f32[256,2048]{1,0:T(8,128)}, u32[]{:S(2)}) copy-start(f32[256,2048]{1,0:T(8,128)} %copy-done.23) | copy-start | bytes 6291460 | tf_op jit(solution)/shard_map/while
  913.0 14.2 %copy-start.33 = (f32[2048,16]{0,1:T(8,128)S(1)}, f32[2048,16]{0,1:T(8,128)}, u32[]{:S(2)}) copy-start(f32[2048,16]{0,1:T(8,128)} %get-tuple-element.1055) | copy-start | bytes 393220 | tf_op jit(solution)/shard_map/while
  913.7 15.2 %copy-start.38 = (f32[256]{0:T(256)S(1)}, f32[256]{0:T(256)}, u32[]{:S(2)}) copy-start(f32[256]{0:T(256)} %get-tuple-element.1086) | copy-start | bytes 3076 | tf_op jit(solution)/shard_map/while
  929.5 15.4 %copy-start.29 = (f32[2048,16]{0,1:T(8,128)S(1)}, f32[2048,16]{0,1:T(8,128)}, u32[]{:S(2)}) copy-start(f32[2048,16]{0,1:T(8,128)} %get-tuple-element.1053) | copy-start | bytes 393220 | tf_op jit(solution)/shard_map/while
  929.5 15.4 %copy-start.31 = (f32[2048,16]{0,1:T(8,128)S(1)}, f32[2048,16]{0,1:T(8,128)}, u32[]{:S(2)}) copy-start(f32[2048,16]{0,1:T(8,128)} %get-tuple-element.1054) | copy-start | bytes 393220 | tf_op jit(solution)/shard_map/while
  930.6 15.7 %copy-start.24 = (f32[256,2048]{1,0:T(8,128)S(1)}, f32[256,2048]{1,0:T(8,128)}, u32[]{:S(2)}) copy-start(f32[256,2048]{1,0:T(8,128)} %copy-done.23) | copy-start | bytes 6291460 | tf_op jit(solution)/shard_map/while
  946.3 6.0 copy-start.23
  964.0 14.2 %copy-start.33 = (f32[2048,16]{0,1:T(8,128)S(1)}, f32[2048,16]{0,1:T(8,128)}, u32[]{:S(2)}) copy-start(f32[2048,16]{0,1:T(8,128)} %get-tuple-element.1055) | copy-start | bytes 393220 | tf_op jit(solution)/shard_map/while
  964.6 15.2 %copy-start.38 = (f32[256]{0:T(256)S(1)}, f32[256]{0:T(256)}, u32[]{:S(2)}) copy-start(f32[256]{0:T(256)} %get-tuple-element.1086) | copy-start | bytes 3076 | tf_op jit(solution)/shard_map/while
  980.4 15.4 %copy-start.29 = (f32[2048,16]{0,1:T(8,128)S(1)}, f32[2048,16]{0,1:T(8,128)}, u32[]{:S(2)}) copy-start(f32[2048,16]{0,1:T(8,128)} %get-tuple-element.1053) | copy-start | bytes 393220 | tf_op jit(solution)/shard_map/while
  980.4 15.4 %copy-start.31 = (f32[2048,16]{0,1:T(8,128)S(1)}, f32[2048,16]{0,1:T(8,128)}, u32[]{:S(2)}) copy-start(f32[2048,16]{0,1:T(8,128)} %get-tuple-element.1054) | copy-start | bytes 393220 | tf_op jit(solution)/shard_map/while
  981.6 15.7 %copy-start.24 = (f32[256,2048]{1,0:T(8,128)S(1)}, f32[256,2048]{1,0:T(8,128)}, u32[]{:S(2)}) copy-start(f32[256,2048]{1,0:T(8,128)} %copy-done.23) | copy-start | bytes 6291460 | tf_op jit(solution)/shard_map/while
  (47 other events, 113.2 us)
Sparse Core Ops, SparseCore 0:
  1000.8 107.5 all-reduce.2
where the time goes:
time: 1130 us; the launch traced here: 1120 us
  waiting for transfers between devices  362 us (32%)
  other arithmetic  254 us (22%)
  blocking collectives  178 us (16%)
  matrix products  136 us (12%)
  local copies, waits for them, and re-layouts  116 us (10%)
  starting transfers between devices  49.9 us (4%)
  between operations  15 us (1%)
    reduce_sum x8, other arithmetic, grad_block(): jnp.sum(real_rows * d_real.reshape(shape_three) + imag_rows * d_imag.resh...  106 us
    psum x1, waiting for transfers between devices, shards(): lax.psum((res_part, rate_part, gain_part), ('ctx', 'dp'))  104 us
    all_to_all x2, waiting for transfers between devices, spectrum(): lax.all_to_all(slot_imag, 'ctx', split_axis=1, concat_axis=1, tiled=True)  83.3 us
    all_to_all x2, waiting for transfers between devices, positions(): lax.all_to_all(out_real, 'ctx', split_axis=1, concat_axis=1, tiled=True)  75.2 us
    psum x1, blocking collectives, shards(): lax.psum((res_part, rate_part, gain_part), ('ctx', 'dp'))  69.5 us
    reduce_sum x4, other arithmetic, kernel_block(): jnp.sum(f_imag.reshape(block, channels, mode_count) * residue, axis=-1)  60.5 us
    all_to_all x1, blocking collectives, transform_plan(): lax.all_to_all(gate_blk.reshape(batch_rows, ctx_count, slice_len, channel...  52.1 us
    all_to_all x1, blocking collectives, transform_plan(): lax.all_to_all(conv_sl, 'ctx', split_axis=1, concat_axis=1, tiled=True)  51.9 us
  transfers between devices with their start and end apart: 11, of which 8 were waited for; matrix products, arithmetic and copies ran while one was open for 36% of the time, Pallas kernels for 0%

commit v1 on v0

--- a/solution.py
+++ b/solution.py
@@ -1,3 +1,4 @@
+import functools
 import math
 import jax
 import jax.numpy as jnp
@@ -7,6 +8,21 @@
 D = 4096
 highest = lax.Precision.HIGHEST
 epsilon = 1e-06
+
+
+def replace_the_target(vector, row_axis):
+    return jnp.concatenate(
+        lax.all_to_all(
+            jnp.stack(jnp.split(vector, lax.axis_size(row_axis), axis=1)),
+            axis_name=row_axis,
+            split_axis=0,
+            concat_axis=0,
+        ),
+        axis=1,
+    )
+
+
+scan_widths = functools.partial(replace_the_target, row_axis="ctx")
 
 
 def modal(decays, angles, parity, seq_len, with_slope):
@@ -96,7 +112,7 @@
         slot_real = jnp.einsum("kb,xbjc->xkjc", forward_real, slices, precision=highest)
         slot_imag = jnp.einsum("kb,xbjc->xkjc", forward_imag, slices, precision=highest)
         rows_real, rows_imag = (
-            lax.all_to_all(slot_real, "ctx", split_axis=1, concat_axis=1, tiled=True),
+            scan_widths(slot_real),
             lax.all_to_all(slot_imag, "ctx", split_axis=1, concat_axis=1, tiled=True),
         )
         rows_real = rows_real.reshape(batch_rows, length, channels)

time: 1130 us -> 1130 us (level)
  local copies, waits for them, and re-layouts: 116 us -> 133 us
    unnamed x62 -> x76, local copies, waits for them, and re-layouts: 13.1 us -> 33.3 us
where the time goes in v1:
time: 1130 us; the launch traced here: 1120 us
  waiting for transfers between devices  354 us (31%)
  other arithmetic  254 us (22%)
  blocking collectives  179 us (16%)
  local copies, waits for them, and re-layouts  133 us (12%)
  matrix products  127 us (11%)
  starting transfers between devices  50 us (4%)
  between operations  15 us (1%)
    reduce_sum x8, other arithmetic, grad_block(): jnp.sum(real_rows * d_real.reshape(shape_three) + imag_rows * d_imag.resh...  106 us
    psum x1, waiting for transfers between devices, shards(): lax.psum((res_part, rate_part, gain_part), ('ctx', 'dp'))  104 us
    all_to_all x2, waiting for transfers between devices, positions(): lax.all_to_all(out_real, 'ctx', split_axis=1, concat_axis=1, tiled=True)  75.1 us
    all_to_all x2, waiting for transfers between devices, spectrum(): lax.all_to_all(slot_imag, 'ctx', split_axis=1, concat_axis=1, tiled=True)  75.1 us
    psum x1, blocking collectives, shards(): lax.psum((res_part, rate_part, gain_part), ('ctx', 'dp'))  69.4 us
    reduce_sum x4, other arithmetic, kernel_block(): jnp.sum(f_imag.reshape(block, channels, mode_count) * residue, axis=-1)  60.5 us
    all_to_all x1, blocking collectives, transform_plan(): lax.all_to_all(gate_blk.reshape(batch_rows, ctx_count, slice_len, channel...  52.2 us
    all_to_all x1, blocking collectives, transform_plan(): lax.all_to_all(conv_sl, 'ctx', split_axis=1, concat_axis=1, tiled=True)  51.9 us
  transfers between devices with their start and end apart: 11, of which 8 were waited for; matrix products, arithmetic and copies ran while one was open for 36% of the time, Pallas kernels for 0%

profile of v1, /device:TPU:0, one launch (start us, length us, event | category | flops | bytes accessed | tf_op | source)
XLA Modules:
  0.0 1117.4 jit_solution(12563380477410278438)
XLA Ops:
  10.1 7.3 all-to-all-start
  21.5 21.6 %all-to-all-done = bf16[1,8,32,2048]{3,2,0,1:T(8,128)(2,1)S(1)} async-done(((bf16[1,8,32,2048]{3,2,0,1:T(8,128)(2,1)}), bf16[1,8,32,2048]{3,2,0,1:T(8,128)(2,1)S(1)}, u32[]{:S(2)}, u32[]{:S(2)}) %all-to-all-start) | async-done | bytes 1048608 | tf_op jit(solution)/shard_map/all_to_all | solution.py:190
  59.5 39.6 %all-to-all-done.2 = f32[1,8,32,2048]{3,2,0,1:T(8,128)S(1)} async-done(((f32[1,8,32,2048]{3,2,0,1:T(8,128)}), f32[1,8,32,2048]{3,2,0,1:T(8,128)S(1)}, u32[]{:S(2)}, u32[]{:S(2)}) %all-to-all-start.2) | async-done | bytes 2097184 | tf_op jit(solution)/shard_map/all_to_all | solution.py:116
  100.5 4.6 all-to-all-start.1
  105.1 114.4 %while.39 = (s32[]{:T(128)}, f32[4,64,2048]{2,1,0:T(8,128)}, f32[4,64,2048]{2,1,0:T(8,128)}, f32[4,64,2048]{2,1,0:T(8,128)}, f32[4,64,2048]{2,1,0:T(8,128)}, /*i...) while((s32[]{:T(128)}, f32[4,64,2048]{2,1,0:T(8,128)}, ...), condition=%wide.region_5.6_spmd, body=%wide.region_0.5_spmd.sunk | while | flops 70910216 | bytes 10621447 | solution.py:185
  116.4 15.1 %fusion.327 = (f32[64,2048]{1,0:T(8,128)S(1)}, f32[64,2048]{1,0:T(8,128)S(1)}, f32[64,2048]{1,0:T(8,128)S(1)}, f32[64,2048]{1,0:T(8,128)S(1)}) fusion(f32[64]{0:T(128)S(1)} %get-tuple-element.922, f32[64]{0:T(128)S(1)} %get-tuple-element.923, f32[2048,16]{0,1:T(8,128)S(1)} %get-tuple-element.1021, f32[2048,16]{0,1:T(8,128)S(1)} %copy.194, ...), kind=kLoop, calls=%fused_computation.19.clone.1 | loop fusion | flops 70778880 | bytes 2884736 | tf_op jit(solution)/shard_map/while/body/eval_jaxpr/reduce_sum | solution.py:181
  145.0 15.1 %fusion.327 = (f32[64,2048]{1,0:T(8,128)S(1)}, f32[64,2048]{1,0:T(8,128)S(1)}, f32[64,2048]{1,0:T(8,128)S(1)}, f32[64,2048]{1,0:T(8,128)S(1)}) fusion(f32[64]{0:T(128)S(1)} %get-tuple-element.922, f32[64]{0:T(128)S(1)} %get-tuple-element.923, f32[2048,16]{0,1:T(8,128)S(1)} %get-tuple-element.1021, f32[2048,16]{0,1:T(8,128)S(1)} %copy.194, ...), kind=kLoop, calls=%fused_computation.19.clone.1 | loop fusion | flops 70778880 | bytes 2884736 | tf_op jit(solution)/shard_map/while/body/eval_jaxpr/reduce_sum | solution.py:181
  173.6 15.1 %fusion.327 = (f32[64,2048]{1,0:T(8,128)S(1)}, f32[64,2048]{1,0:T(8,128)S(1)}, f32[64,2048]{1,0:T(8,128)S(1)}, f32[64,2048]{1,0:T(8,128)S(1)}) fusion(f32[64]{0:T(128)S(1)} %get-tuple-element.922, f32[64]{0:T(128)S(1)} %get-tuple-element.923, f32[2048,16]{0,1:T(8,128)S(1)} %get-tuple-element.1021, f32[2048,16]{0,1:T(8,128)S(1)} %copy.194, ...), kind=kLoop, calls=%fused_computation.19.clone.1 | loop fusion | flops 70778880 | bytes 2884736 | tf_op jit(solution)/shard_map/while/body/eval_jaxpr/reduce_sum | solution.py:181
  202.2 15.1 %fusion.327 = (f32[64,2048]{1,0:T(8,128)S(1)}, f32[64,2048]{1,0:T(8,128)S(1)}, f32[64,2048]{1,0:T(8,128)S(1)}, f32[64,2048]{1,0:T(8,128)S(1)}) fusion(f32[64]{0:T(128)S(1)} %get-tuple-element.922, f32[64]{0:T(128)S(1)} %get-tuple-element.923, f32[2048,16]{0,1:T(8,128)S(1)} %get-tuple-element.1021, f32[2048,16]{0,1:T(8,128)S(1)} %copy.194, ...), kind=kLoop, calls=%fused_computation.19.clone.1 | loop fusion | flops 70778880 | bytes 2884736 | tf_op jit(solution)/shard_map/while/body/eval_jaxpr/reduce_sum | solution.py:181
  230.6 5.9 convolution_bitcast_fusion.7
  244.2 6.1 multiply_subtract_fusion.2
  250.4 5.8 multiply_add_fusion.6
  259.5 4.8 convolution_subtract_fusion.1
  264.3 6.1 all-to-all-start.3
  270.4 4.9 fusion.51
  275.4 4.7 convolution_add_fusion.3
  280.0 37.6 %all-to-all-done.3 = f32[1,8,32,2048]{3,2,0,1:T(8,128)} async-done(((f32[1,8,32,2048]{3,2,0,1:T(8,128)}), f32[1,8,32,2048]{3,2,0,1:T(8,128)}, u32[]{:S(2)}, u32[]{:S(2)}) %all-to-all-start.3) | async-done | bytes 2097184 | tf_op jit(solution)/shard_map/all_to_all | solution.py:143
  321.8 6.2 fusion.68
  327.9 42.2 %all-to-all-done.4 = f32[1,8,32,2048]{3,2,0,1:T(8,128)S(1)} async-done(((f32[1,8,32,2048]{3,2,0,1:T(8,128)}), f32[1,8,32,2048]{3,2,0,1:T(8,128)S(1)}, u32[]{:S(2)}, u32[]{:S(2)}) %all-to-all-start.4) | async-done | bytes 2097184 | tf_op jit(solution)/shard_map/all_to_all | solution.py:144
  370.1 4.9 fusion.37
  376.2 51.9 %all_to_all.60 = f32[1,8,32,2048]{3,2,0,1:T(8,128)S(1)} all-to-all(f32[1,8,32,2048]{3,2,0,1:T(8,128)S(1)} %copy.126), channel_id=1, replica_groups=mesh['ctx'=8,'chan'=2,'dp'=2] {'ctx'}, dimensions={1} | all-to-all | bytes 4194304 | tf_op jit(solution)/shard_map/all_to_all | solution.py:199
  439.0 52.2 %all_to_all.61 = f32[1,8,32,2048]{3,2,0,1:T(8,128)} all-to-all(f32[1,8,32,2048]{3,2,0,1:T(8,128)S(1)} %bitcast.282), channel_id=1, replica_groups=mesh['ctx'=8,'chan'=2,'dp'=2] {'ctx'}, dimensions={1} | all-to-all | bytes 4194304 | tf_op jit(solution)/shard_map/all_to_all | solution.py:203
  491.2 4.8 convolution_bitcast_fusion.2
  502.2 4.8 convolution_bitcast_fusion.5
  514.5 35.6 %all-to-all-done.8 = f32[1,8,32,2048]{3,2,0,1:T(8,128)S(1)} async-done(((f32[1,8,32,2048]{3,2,0,1:T(8,128)}), f32[1,8,32,2048]{3,2,0,1:T(8,128)S(1)}, u32[]{:S(2)}, u32[]{:S(2)}) %all-to-all-start.8) | async-done | bytes 2097184 | tf_op jit(solution)/shard_map/all_to_all | solution.py:116
  550.1 4.6 all-to-all-start.7
  554.6 5.6 convolution_bitcast_fusion
  560.3 5.7 convolution_bitcast_fusion.1
  566.0 36.3 %all-to-all-done.7 = f32[8,1,1,32,2048]{4,1,3,2,0:T(1,128)} async-done(((f32[8,1,1,32,2048]{4,1,3,2,0:T(1,128)}), f32[8,1,1,32,2048]{4,1,3,2,0:T(1,128)}, u32[]{:S(2)}, u32[]{:S(2)}) %all-to-all-start.7) | async-done | bytes 2097184 | tf_op jit(solution)/shard_map/all_to_all | solution.py:15
  604.7 5.9 convolution_bitcast_fusion.3
  610.6 17.0 %subtract_bitcast_fusion.1 = (f32[256,2048]{0,1:T(8,128)}, f32[256,2048]{0,1:T(8,128)}, f32[256,2048]{0,1:T(8,128)}, f32[256,2048]{0,1:T(8,128)}, f32[1,256,2048...) fusion(f32[1,256,2048]{1,2,0:T(8,128)} %copy-done.7, ...), kind=kOutput, calls=%fused_computation.170 | convolution fusion | flops 1630928896 | bytes 41944064 | tf_op jit(solution)/shard_map/kj,xjc->xkc/dot_general | solution.py:120
  639.9 5.6 fusion.56
  645.4 4.7 convolution_add_fusion.1
  650.1 37.5 %all-to-all-done.9 = f32[1,8,32,2048]{3,2,0,1:T(8,128)} async-done(((f32[1,8,32,2048]{3,2,0,1:T(8,128)}), f32[1,8,32,2048]{3,2,0,1:T(8,128)}, u32[]{:S(2)}, u32[]{:S(2)}) %all-to-all-start.9) | async-done | bytes 2097184 | tf_op jit(solution)/shard_map/all_to_all | solution.py:143
  692.1 69.4 %psum.39 = f32[2048]{0:T(1024)} all-reduce(f32[2048]{0:T(1024)S(1)} %get-tuple-element.596), channel_id=1, replica_groups=mesh['ctx'=8,'chan'=2,'dp'=2] {'ctx','dp'}, use_global_device_ids=true, to_apply=%region_19.20 | all-reduce | flops 2048 | bytes 16384 | tf_op jit(solution)/shard_map/psum | solution.py:279
  771.4 6.2 fusion.60
  777.5 5.5 fusion.36
  785.6 7.2 all-to-all-start.11
  793.4 202.4 %while.40 = (s32[]{:T(128)}, f32[2048,16]{0,1:T(8,128)}, f32[2048,16]{0,1:T(8,128)}, f32[2048,16]{0,1:T(8,128)}, f32[2048,16]{0,1:T(8,128)}, /*index=5*/s32[4]{0...) while((s32[]{:T(128)}, f32[2048,16]{0,1:T(8,128)}, ...), condition=%wide.region_15.16_spmd.clone, body=%wide.region_10.15_spmd.clone.sunk | while | flops 180650240 | bytes 40907724 | solution.py:268
  811.7 13.6 %add_reduce_fusion.8 = (f32[2048,16]{0,1:T(8,128)S(1)}, f32[2048,16]{0,1:T(8,128)S(1)}) fusion(f32[64]{0:T(128)S(1)} %get-tuple-element.965, f32[64,2048]{1,0:T(8,128)S(1)} %copy-done, f32[64]{0:T(128)S(1)} %get-tuple-element.966, f32[64]{0:T(128)S(1)} %get-tuple-element.967, f32[64,2048]{1,0:T(8,128)S(1)} %copy-done.1, f32[2048,16]{0,1:T(8,128)S(1)} %copy.199, ...), kind=kLoop, calls=%fused_computation.71.clone.1 | loop fusion | flops 90112000 | bytes 2360128 | tf_op jit(solution)/shard_map/while/body/eval_jaxpr/reduce_sum | solution.py:259
  829.2 12.9 %add_reduce_fusion.7 = (f32[2048,16]{0,1:T(8,128)S(1)}, f32[2048,16]{0,1:T(8,128)S(1)}) fusion(f32[2048,16]{0,1:T(8,128)S(1)} %copy.199, f32[64]{0:T(128)S(1)} %get-tuple-element.954, f32[2048,16]{0,1:T(8,128)S(1)} %copy.200, f32[2048,16]{0,1:T(8,128)S(1)} %copy.201, f32[64,2048]{1,0:T(8,128)S(1)} %constant_dynamic-slice_fusion.8, ...), kind=kLoop, calls=%fused_computation.75.clone.1 | loop fusion | flops 90112000 | bytes 2360128 | tf_op jit(solution)/shard_map/while/body/eval_jaxpr/reduce_sum | solution.py:259
  861.6 13.6 %add_reduce_fusion.8 = (f32[2048,16]{0,1:T(8,128)S(1)}, f32[2048,16]{0,1:T(8,128)S(1)}) fusion(f32[64]{0:T(128)S(1)} %get-tuple-element.965, f32[64,2048]{1,0:T(8,128)S(1)} %copy-done, f32[64]{0:T(128)S(1)} %get-tuple-element.966, f32[64]{0:T(128)S(1)} %get-tuple-element.967, f32[64,2048]{1,0:T(8,128)S(1)} %copy-done.1, f32[2048,16]{0,1:T(8,128)S(1)} %copy.199, ...), kind=kLoop, calls=%fused_computation.71.clone.1 | loop fusion | flops 90112000 | bytes 2360128 | tf_op jit(solution)/shard_map/while/body/eval_jaxpr/reduce_sum | solution.py:259
  880.0 12.9 %add_reduce_fusion.7 = (f32[2048,16]{0,1:T(8,128)S(1)}, f32[2048,16]{0,1:T(8,128)S(1)}) fusion(f32[2048,16]{0,1:T(8,128)S(1)} %copy.199, f32[64]{0:T(128)S(1)} %get-tuple-element.954, f32[2048,16]{0,1:T(8,128)S(1)} %copy.200, f32[2048,16]{0,1:T(8,128)S(1)} %copy.201, f32[64,2048]{1,0:T(8,128)S(1)} %constant_dynamic-slice_fusion.8, ...), kind=kLoop, calls=%fused_computation.75.clone.1 | loop fusion | flops 90112000 | bytes 2360128 | tf_op jit(solution)/shard_map/while/body/eval_jaxpr/reduce_sum | solution.py:259
  912.4 13.6 %add_reduce_fusion.8 = (f32[2048,16]{0,1:T(8,128)S(1)}, f32[2048,16]{0,1:T(8,128)S(1)}) fusion(f32[64]{0:T(128)S(1)} %get-tuple-element.965, f32[64,2048]{1,0:T(8,128)S(1)} %copy-done, f32[64]{0:T(128)S(1)} %get-tuple-element.966, f32[64]{0:T(128)S(1)} %get-tuple-element.967, f32[64,2048]{1,0:T(8,128)S(1)} %copy-done.1, f32[2048,16]{0,1:T(8,128)S(1)} %copy.199, ...), kind=kLoop, calls=%fused_computation.71.clone.1 | loop fusion | flops 90112000 | bytes 2360128 | tf_op jit(solution)/shard_map/while/body/eval_jaxpr/reduce_sum | solution.py:259
  930.7 12.9 %add_reduce_fusion.7 = (f32[2048,16]{0,1:T(8,128)S(1)}, f32[2048,16]{0,1:T(8,128)S(1)}) fusion(f32[2048,16]{0,1:T(8,128)S(1)} %copy.199, f32[64]{0:T(128)S(1)} %get-tuple-element.954, f32[2048,16]{0,1:T(8,128)S(1)} %copy.200, f32[2048,16]{0,1:T(8,128)S(1)} %copy.201, f32[64,2048]{1,0:T(8,128)S(1)} %constant_dynamic-slice_fusion.8, ...), kind=kLoop, calls=%fused_computation.75.clone.1 | loop fusion | flops 90112000 | bytes 2360128 | tf_op jit(solution)/shard_map/while/body/eval_jaxpr/reduce_sum | solution.py:259
  963.2 13.6 %add_reduce_fusion.8 = (f32[2048,16]{0,1:T(8,128)S(1)}, f32[2048,16]{0,1:T(8,128)S(1)}) fusion(f32[64]{0:T(128)S(1)} %get-tuple-element.965, f32[64,2048]{1,0:T(8,128)S(1)} %copy-done, f32[64]{0:T(128)S(1)} %get-tuple-element.966, f32[64]{0:T(128)S(1)} %get-tuple-element.967, f32[64,2048]{1,0:T(8,128)S(1)} %copy-done.1, f32[2048,16]{0,1:T(8,128)S(1)} %copy.199, ...), kind=kLoop, calls=%fused_computation.71.clone.1 | loop fusion | flops 90112000 | bytes 2360128 | tf_op jit(solution)/shard_map/while/body/eval_jaxpr/reduce_sum | solution.py:259
  981.5 12.9 %add_reduce_fusion.7 = (f32[2048,16]{0,1:T(8,128)S(1)}, f32[2048,16]{0,1:T(8,128)S(1)}) fusion(f32[2048,16]{0,1:T(8,128)S(1)} %copy.199, f32[64]{0:T(128)S(1)} %get-tuple-element.954, f32[2048,16]{0,1:T(8,128)S(1)} %copy.200, f32[2048,16]{0,1:T(8,128)S(1)} %copy.201, f32[64,2048]{1,0:T(8,128)S(1)} %constant_dynamic-slice_fusion.8, ...), kind=kLoop, calls=%fused_computation.75.clone.1 | loop fusion | flops 90112000 | bytes 2360128 | tf_op jit(solution)/shard_map/while/body/eval_jaxpr/reduce_sum | solution.py:259
  1003.4 103.6 %all-reduce.3.cloned.1.call-done = (f32[2048,16]{0,1:T(8,128)}, f32[2048,16]{0,1:T(8,128)}) async-done(((f32[2048,16]{0,1:T(8,128)}, f32[2048,16]{0,1:T(8,128)}), (f32[2048,16]{0,1:T(8,128)}, f32[2048,16]{0,1:T(8,128)})) %all-reduce.3.cloned.1.call-update) | async-done | bytes 262160 | tf_op jit(solution)/shard_map/psum | solution.py:279
  (453 shorter events, 262.9 us)
Async XLA Ops:
  7.2 10.2 copy-start.35
  10.1 33.0 %all-to-all-start = ((bf16[1,8,32,2048]{3,2,0,1:T(8,128)(2,1)}), bf16[1,8,32,2048]{3,2,0,1:T(8,128)(2,1)S(1)}, u32[]{:S(2)}, u32[]{:S(2)}) async-start(bf16[1,8,32,2048]{3,2,0,1:T(8,128)(2,1)} %bitcast.6), calls=%async_computation | async-start | bytes 2097152 | tf_op jit(solution)/shard_map/all_to_all | solution.py:190
  47.1 52.0 %all-to-all-start.2 = ((f32[1,8,32,2048]{3,2,0,1:T(8,128)}), f32[1,8,32,2048]{3,2,0,1:T(8,128)S(1)}, u32[]{:S(2)}, u32[]{:S(2)}) async-start(f32[1,8,32,2048]{3,2,0,1:T(8,128)} %copy.115), calls=%async_computation.2 | async-start | bytes 4194304 | tf_op jit(solution)/shard_map/all_to_all | solution.py:116
  59.5 45.6 %copy-start.26 = (f32[2048,16]{0,1:T(8,128)S(1)}, f32[2048,16]{0,1:T(8,128)}, u32[]{:S(2)}) copy-start(f32[2048,16]{0,1:T(8,128)} %param.16) | copy-start | bytes 393220
  100.5 136.1 %all-to-all-start.1 = ((f32[8,1,1,32,2048]{4,1,3,2,0:T(1,128)}), f32[8,1,1,32,2048]{4,1,3,2,0:T(1,128)}, u32[]{:S(2)}, u32[]{:S(2)}) async-start(f32[8,1,1,32,2048]{4,1,3,2,0:T(1,128)} %fusion.114), calls=%async_computation.1 | async-start | bytes 4194304 | tf_op jit(solution)/shard_map/all_to_all | solution.py:15
  236.5 13.8 %copy-start.6 = (f32[1,256,2048]{1,2,0:T(8,128)}, f32[1,256,2048]{1,2,0:T(8,128)S(1)}, u32[]{:S(2)}) copy-start(f32[1,256,2048]{1,2,0:T(8,128)S(1)} %convolution_bitcast_fusion.7) | copy-start | bytes 6291460
  236.6 7.6 copy-start.20
  244.2 6.1 copy-start.7
  244.2 6.1 copy-start.10
  244.2 6.1 copy-start.11
  250.3 5.9 copy-start.12
  250.4 9.1 copy-start.14
  264.3 6.1 copy-start.15
  264.3 53.4 %all-to-all-start.3 = ((f32[1,8,32,2048]{3,2,0,1:T(8,128)}), f32[1,8,32,2048]{3,2,0,1:T(8,128)}, u32[]{:S(2)}, u32[]{:S(2)}) async-start(f32[1,8,32,2048]{3,2,0,1:T(8,128)} %bitcast.281), calls=%async_computation.3 | async-start | bytes 4194304 | tf_op jit(solution)/shard_map/all_to_all | solution.py:143
  317.7 52.4 %all-to-all-start.4 = ((f32[1,8,32,2048]{3,2,0,1:T(8,128)}), f32[1,8,32,2048]{3,2,0,1:T(8,128)S(1)}, u32[]{:S(2)}, u32[]{:S(2)}) async-start(f32[1,8,32,2048]{3,2,0,1:T(8,128)} %bitcast.52), calls=%async_computation.4 | async-start | bytes 4194304 | tf_op jit(solution)/shard_map/all_to_all | solution.py:144
  376.2 52.0 %copy-start.24 = (bf16[1,256,2048]{2,1,0:T(8,128)(2,1)S(1)}, bf16[1,256,2048]{2,1,0:T(8,128)(2,1)}, u32[]{:S(2)}) copy-start(bf16[1,256,2048]{2,1,0:T(8,128)(2,1)} %param.11) | copy-start | bytes 3145732
  498.5 51.5 %all-to-all-start.8 = ((f32[1,8,32,2048]{3,2,0,1:T(8,128)}), f32[1,8,32,2048]{3,2,0,1:T(8,128)S(1)}, u32[]{:S(2)}, u32[]{:S(2)}) async-start(f32[1,8,32,2048]{3,2,0,1:T(8,128)} %copy.131), calls=%async_computation.8 | async-start | bytes 4194304 | tf_op jit(solution)/shard_map/all_to_all | solution.py:116
  550.1 52.2 %all-to-all-start.7 = ((f32[8,1,1,32,2048]{4,1,3,2,0:T(1,128)}), f32[8,1,1,32,2048]{4,1,3,2,0:T(1,128)}, u32[]{:S(2)}, u32[]{:S(2)}) async-start(f32[8,1,1,32,2048]{4,1,3,2,0:T(1,128)} %fusion.106), calls=%async_computation.7 | async-start | bytes 4194304 | tf_op jit(solution)/shard_map/all_to_all | solution.py:15
  627.6 7.7 copy-start.4
  627.6 7.7 copy-start.5
  635.3 52.3 %all-to-all-start.9 = ((f32[1,8,32,2048]{3,2,0,1:T(8,128)}), f32[1,8,32,2048]{3,2,0,1:T(8,128)}, u32[]{:S(2)}, u32[]{:S(2)}) async-start(f32[1,8,32,2048]{3,2,0,1:T(8,128)} %bitcast.280), calls=%async_computation.9 | async-start | bytes 4194304 | tf_op jit(solution)/shard_map/all_to_all | solution.py:143
  687.7 89.9 %all-to-all-start.10 = ((f32[1,8,32,2048]{3,2,0,1:T(8,128)}), f32[1,8,32,2048]{3,2,0,1:T(8,128)}, u32[]{:S(2)}, u32[]{:S(2)}) async-start(f32[1,8,32,2048]{3,2,0,1:T(8,128)} %bitcast.279), calls=%async_computation.10 | async-start | bytes 4194304 | tf_op jit(solution)/shard_map/all_to_all | solution.py:144
  785.6 213.7 %all-to-all-start.11 = ((f32[1,8,32,2048]{3,2,0,1:T(8,128)}), f32[1,8,32,2048]{3,2,0,1:T(8,128)}, u32[]{:S(2)}, u32[]{:S(2)}) async-start(f32[1,8,32,2048]{3,2,0,1:T(8,128)} %copy.142), calls=%async_computation.11 | async-start | bytes 4194304 | tf_op jit(solution)/shard_map/all_to_all | solution.py:212
  792.8 314.2 %all-reduce.3.cloned.1.call-start = ((), (), s32[]{:S(2)}) async-start(), calls=%async_computation.12 | async-start | bytes 524288 | tf_op jit(solution)/shard_map/psum | solution.py:279
  793.6 6.0 copy-start.22
  811.1 14.3 %copy-start.32 = (f32[2048,16]{0,1:T(8,128)S(1)}, f32[2048,16]{0,1:T(8,128)}, u32[]{:S(2)}) copy-start(f32[2048,16]{0,1:T(8,128)} %get-tuple-element.1055) | copy-start | bytes 393220 | tf_op jit(solution)/shard_map/while
  811.7 14.4 %copy-start.37 = (f32[256]{0:T(256)S(1)}, f32[256]{0:T(256)}, u32[]{:S(2)}) copy-start(f32[256]{0:T(256)} %get-tuple-element.1086) | copy-start | bytes 3076 | tf_op jit(solution)/shard_map/while
  826.7 15.4 %copy-start.28 = (f32[2048,16]{0,1:T(8,128)S(1)}, f32[2048,16]{0,1:T(8,128)}, u32[]{:S(2)}) copy-start(f32[2048,16]{0,1:T(8,128)} %get-tuple-element.1053) | copy-start | bytes 393220 | tf_op jit(solution)/shard_map/while
  826.7 15.4 %copy-start.30 = (f32[2048,16]{0,1:T(8,128)S(1)}, f32[2048,16]{0,1:T(8,128)}, u32[]{:S(2)}) copy-start(f32[2048,16]{0,1:T(8,128)} %get-tuple-element.1054) | copy-start | bytes 393220 | tf_op jit(solution)/shard_map/while
  827.8 15.6 %copy-start.23 = (f32[256,2048]{1,0:T(8,128)S(1)}, f32[256,2048]{1,0:T(8,128)}, u32[]{:S(2)}) copy-start(f32[256,2048]{1,0:T(8,128)} %copy-done.22) | copy-start | bytes 6291460 | tf_op jit(solution)/shard_map/while
  843.5 6.0 copy-start.22
  860.9 14.3 %copy-start.32 = (f32[2048,16]{0,1:T(8,128)S(1)}, f32[2048,16]{0,1:T(8,128)}, u32[]{:S(2)}) copy-start(f32[2048,16]{0,1:T(8,128)} %get-tuple-element.1055) | copy-start | bytes 393220 | tf_op jit(solution)/shard_map/while
  861.6 15.3 %copy-start.37 = (f32[256]{0:T(256)S(1)}, f32[256]{0:T(256)}, u32[]{:S(2)}) copy-start(f32[256]{0:T(256)} %get-tuple-element.1086) | copy-start | bytes 3076 | tf_op jit(solution)/shard_map/while
  877.5 15.4 %copy-start.28 = (f32[2048,16]{0,1:T(8,128)S(1)}, f32[2048,16]{0,1:T(8,128)}, u32[]{:S(2)}) copy-start(f32[2048,16]{0,1:T(8,128)} %get-tuple-element.1053) | copy-start | bytes 393220 | tf_op jit(solution)/shard_map/while
  877.5 15.4 %copy-start.30 = (f32[2048,16]{0,1:T(8,128)S(1)}, f32[2048,16]{0,1:T(8,128)}, u32[]{:S(2)}) copy-start(f32[2048,16]{0,1:T(8,128)} %get-tuple-element.1054) | copy-start | bytes 393220 | tf_op jit(solution)/shard_map/while
  878.6 15.6 %copy-start.23 = (f32[256,2048]{1,0:T(8,128)S(1)}, f32[256,2048]{1,0:T(8,128)}, u32[]{:S(2)}) copy-start(f32[256,2048]{1,0:T(8,128)} %copy-done.22) | copy-start | bytes 6291460 | tf_op jit(solution)/shard_map/while
  894.3 6.0 copy-start.22
  911.7 14.3 %copy-start.32 = (f32[2048,16]{0,1:T(8,128)S(1)}, f32[2048,16]{0,1:T(8,128)}, u32[]{:S(2)}) copy-start(f32[2048,16]{0,1:T(8,128)} %get-tuple-element.1055) | copy-start | bytes 393220 | tf_op jit(solution)/shard_map/while
  912.4 15.3 %copy-start.37 = (f32[256]{0:T(256)S(1)}, f32[256]{0:T(256)}, u32[]{:S(2)}) copy-start(f32[256]{0:T(256)} %get-tuple-element.1086) | copy-start | bytes 3076 | tf_op jit(solution)/shard_map/while
  928.3 15.4 %copy-start.28 = (f32[2048,16]{0,1:T(8,128)S(1)}, f32[2048,16]{0,1:T(8,128)}, u32[]{:S(2)}) copy-start(f32[2048,16]{0,1:T(8,128)} %get-tuple-element.1053) | copy-start | bytes 393220 | tf_op jit(solution)/shard_map/while
  928.3 15.4 %copy-start.30 = (f32[2048,16]{0,1:T(8,128)S(1)}, f32[2048,16]{0,1:T(8,128)}, u32[]{:S(2)}) copy-start(f32[2048,16]{0,1:T(8,128)} %get-tuple-element.1054) | copy-start | bytes 393220 | tf_op jit(solution)/shard_map/while
  929.4 15.6 %copy-start.23 = (f32[256,2048]{1,0:T(8,128)S(1)}, f32[256,2048]{1,0:T(8,128)}, u32[]{:S(2)}) copy-start(f32[256,2048]{1,0:T(8,128)} %copy-done.22) | copy-start | bytes 6291460 | tf_op jit(solution)/shard_map/while
  945.0 6.0 copy-start.22
  962.5 14.3 %copy-start.32 = (f32[2048,16]{0,1:T(8,128)S(1)}, f32[2048,16]{0,1:T(8,128)}, u32[]{:S(2)}) copy-start(f32[2048,16]{0,1:T(8,128)} %get-tuple-element.1055) | copy-start | bytes 393220 | tf_op jit(solution)/shard_map/while
  963.1 15.3 %copy-start.37 = (f32[256]{0:T(256)S(1)}, f32[256]{0:T(256)}, u32[]{:S(2)}) copy-start(f32[256]{0:T(256)} %get-tuple-element.1086) | copy-start | bytes 3076 | tf_op jit(solution)/shard_map/while
  979.0 15.4 %copy-start.28 = (f32[2048,16]{0,1:T(8,128)S(1)}, f32[2048,16]{0,1:T(8,128)}, u32[]{:S(2)}) copy-start(f32[2048,16]{0,1:T(8,128)} %get-tuple-element.1053) | copy-start | bytes 393220 | tf_op jit(solution)/shard_map/while
  979.1 15.4 %copy-start.30 = (f32[2048,16]{0,1:T(8,128)S(1)}, f32[2048,16]{0,1:T(8,128)}, u32[]{:S(2)}) copy-start(f32[2048,16]{0,1:T(8,128)} %get-tuple-element.1054) | copy-start | bytes 393220 | tf_op jit(solution)/shard_map/while
  980.2 15.6 %copy-start.23 = (f32[256,2048]{1,0:T(8,128)S(1)}, f32[256,2048]{1,0:T(8,128)}, u32[]{:S(2)}) copy-start(f32[256,2048]{1,0:T(8,128)} %copy-done.22) | copy-start | bytes 6291460 | tf_op jit(solution)/shard_map/while
  (46 other events, 100.5 us)
Sparse Core Ops, SparseCore 0:
  999.4 107.5 all-reduce.2
